TPU v7x, 32 devices: a whole 2x2x4 slice. The times are simulated.
32 devices in a mesh: fsdp: 8 (over z, x), tensor: 2 (over y), dp: 2 (over core).
Axes of the slice: x: 2, y: 2, z: 4, core: 2. Of those that a mesh axis runs over, the one named last changes fastest.
Arguments:
- states: bfloat16 [4096, 4096], P('fsdp', ('tensor', 'dp')), may hold values from -6 to 6
- fresh_rows: bfloat16 [4096, 4096], P('fsdp', ('tensor', 'dp')), may hold values from -6 to 6
- norm_gain: bfloat16 [4096], P(('tensor', 'dp')), may hold values from 0.25 to 1.75
- gate_weight: bfloat16 [4096, 8192], P('fsdp', ('tensor', 'dp')), may hold values from -0.09375 to 0.09375
- up_weight: bfloat16 [4096, 8192], P('fsdp', ('tensor', 'dp')), may hold values from -0.09375 to 0.09375
- down_weight: bfloat16 [8192, 4096], P(('tensor', 'dp'), 'fsdp'), may hold values from -0.09375 to 0.09375
- halted: int32 [64, 64], P('fsdp'), may hold values from 0 to 1, as said below
- refill_index: int32 [64, 64], P('fsdp'), may hold values from 0 to 63, each once within a row
Outputs:
- next_states: bfloat16 [4096, 4096], P('fsdp', ('tensor', 'dp'))
Inputs may be any that keep to these rules, and one draw needn't show every extreme that they name: In each aligned block of 512 rows (in row order over all batches) at most 384 rows are running (halted 0), and some block has exactly 384 running rows. Each batch's row of refill_index holds every number of 0 to 63 once.
All inputs are finite; a program needn't handle non-finite values.
Results may differ from a plain program's by a relative error of at most 0.0085.
Values may be sent and summed in bfloat16 or wider, within the bound.
A program may use at most 128 MiB of HBM per device.

v0:
```python
import functools

import jax
import jax.numpy as jnp
from jax import lax
from jax.experimental import pallas as pl
from jax.experimental.pallas import tpu as pltpu
from jax.sharding import PartitionSpec as P

MESH = pl.DeviceIdType.MESH
norm_eps = 1e-05


class Plan:
    def __init__(self, mesh, states, gate, down):
        self.F, self.T, self.C = (mesh.shape[axis] for axis in ("fsdp", "tensor", "dp"))
        self.R = min(4, max(1, self.F // 2))
        self.S = self.F // self.R
        self.K = self.T * self.C
        self.unit = self.F // self.K
        self.rows, self.width = states.shape
        self.cap = self.rows * 3 // 4
        self.features = self.width * self.K
        self.fw = gate.shape[0]
        self.hp = gate.shape[1] // self.R
        self.halves = 2 if self.fw % 256 == 0 else 1
        self.pw = self.fw // self.halves
        self.mats = 2 + self.halves
        self.parts = self.unit * self.halves


def block_kernel(
    p,
    pick_row, pick_col, fill_col, states, fresh, gain, gate_w, up_w, down_w,
    out,
    rows, gate_full, up_full, down_full, gate_acc, up_acc, hidden, kept, ms_c, ms_t,
    crecv, yrecv, zrecv, mine,
    local_sem, gz_send, gz_recv, xs_send, xs_recv, rz_send, rz_recv, ry_send, ry_recv,
    rc_send, rc_recv, mc_send, mc_recv, mt_send, mt_recv,
    oc_send, oc_recv, oy_send, oy_recv, oz_send, oz_recv,
):
    R, S, T, C, K = p.R, p.S, p.T, p.C, p.K
    cap, width, fw, hp, pw = p.cap, p.width, p.fw, p.hp, p.pw
    f, t, c = lax.axis_index("fsdp"), lax.axis_index("tensor"), lax.axis_index("dp")
    a, b = f // S, f % S
    me = t * C + c

    def remote(src, dst, send_sem, recv_sem, axis, index):
        return pltpu.make_async_remote_copy(
            src_ref=src, dst_ref=dst, send_sem=send_sem, recv_sem=recv_sem,
            device_id={axis: index}, device_id_type=MESH,
        )

    def when(cond, run):
        if cond is True:
            run()
        else:
            pl.when(cond)(run)

    def both(one, two):
        return two if one is True else jnp.logical_and(one, two)

    sent = []

    def send(make, cond=True, log=None):
        when(cond, lambda: make().start())
        (sent if log is None else log).append((make, cond))

    def near(step):
        return [(a - step, a >= step), (a + step, a + step < R)]

    by_distance = [(a, True)] + [pair for step in range(1, R) for pair in near(step)]
    arrivals = by_distance[1:]

    def source_at(m, to):
        if m < 2:
            return (gate_w, up_w)[m].at[:, pl.ds(pl.multiple_of(to * hp, hp), hp)]
        h = m - 2
        return down_w.at[pl.ds(pl.multiple_of(to * hp, hp), hp), h * pw : (h + 1) * pw]

    def full_at(m, owner):
        if m < 2:
            return (gate_full, up_full)[m].at[pl.ds(pl.multiple_of(owner * fw, fw), fw), :]
        return down_full.at[m - 2, owner]

    def send_z(m):
        for step in range(R - 1, 0, -1):
            for to, cond in near(step):
                send(
                    lambda m=m, to=to: remote(
                        source_at(m, to), full_at(m, f), gz_send.at[m, to], gz_recv.at[m, a],
                        "fsdp", to * S + b,
                    ),
                    cond,
                )

    def wait_z(m, frm):
        place = full_at(m, frm * S + b)
        remote(place, place, gz_send.at[m, frm], gz_recv.at[m, frm], "fsdp", frm * S + b).wait_recv()

    def send_x(m, frm, cond, own=False):
        for step in range(1, S):
            def make(m=m, frm=frm, step=step):
                place = full_at(m, frm * S + b)
                return remote(
                    source_at(m, a) if own else place, place,
                    xs_send.at[m, frm, step], xs_recv.at[m, frm, step],
                    "fsdp", a * S + (b + step) % S,
                )
            send(make, cond)

    def wait_x(m, frm, step):
        owner = (b + S - step) % S
        place = full_at(m, frm * S + owner)
        remote(
            place, place, xs_send.at[m, frm, step], xs_recv.at[m, frm, step], "fsdp", a * S + owner
        ).wait_recv()

    def local(m):
        return pltpu.make_async_copy(source_at(m, a), full_at(m, f), local_sem.at[m])

    def forward_z(m, pairs):
        for frm, cond in pairs:
            when(cond, lambda frm=frm: wait_z(m, frm))
            send_x(m, frm, cond)

    barrier = pltpu.get_barrier_semaphore()
    partners = [("fsdp", ((a + step) % R) * S + b) for step in range(1, R)]
    partners += [("fsdp", a * S + (b + step) % S) for step in range(1, S)]
    partners += [("tensor", (t + step) % T) for step in range(1, T)]
    partners += [("dp", (c + step) % C) for step in range(1, C)]
    for axis, index in partners:
        pl.semaphore_signal(barrier, inc=1, device_id={axis: index}, device_id_type=MESH)
    pl.semaphore_wait(barrier, len(partners))

    send_z(0)
    send_x(0, a, True, own=True)
    for m in range(p.mats):
        local(m).start()

    ids = lax.broadcasted_iota(jnp.int32, (cap, p.rows), 0)
    picker = (ids == pick_row[...]).astype(jnp.bfloat16)
    picked = jnp.dot(picker, states[...], preferred_element_type=jnp.float32)
    kept[...] = picked.astype(jnp.bfloat16)
    ms_c[c] = jnp.broadcast_to(jnp.sum(picked * picked, axis=-1, keepdims=True), (cap, 128))

    def exchange(buffer, own, axis, count, send_sem, recv_sem):
        def copy(step):
            return remote(
                buffer.at[own], buffer.at[own], send_sem.at[step], recv_sem.at[step],
                axis, (own + step) % count,
            )
        for step in range(1, count):
            send(lambda step=step: copy(step))
        for step in range(1, count):
            place = buffer.at[(own + count - step) % count]
            remote(
                place, place, send_sem.at[step], recv_sem.at[step], axis, (own + count - step) % count
            ).wait_recv()
        return functools.reduce(lambda one, two: one + two, [buffer[k] for k in range(count)])

    ms_t[t] = exchange(ms_c, c, "dp", C, mc_send, mc_recv)
    total_square = exchange(ms_t, t, "tensor", T, mt_send, mt_recv)[:, :1]
    scale = lax.rsqrt(total_square / p.features + norm_eps)
    rows[me, a] = (
        kept[...].astype(jnp.float32) * scale * gain[...].astype(jnp.float32)
    ).astype(jnp.bfloat16)

    row_sent = []

    def row_z(slot, move, cond):
        way = 0 if move > 0 else 1
        place = lambda: rows.at[me, slot]
        send(
            lambda: remote(
                place(), place(), rz_send.at[way, slot], rz_recv.at[slot], "fsdp", (a + move) * S + b
            ),
            cond, row_sent,
        )

    def row_wait_z(slot):
        place = rows.at[me, slot]
        remote(place, place, rz_send.at[0, slot], rz_recv.at[slot], "fsdp", ((a + 1) % R) * S + b).wait_recv()

    def row_y(slot, cond):
        for step in range(1, T):
            send(
                lambda step=step: remote(
                    rows.at[me, slot], rows.at[me, slot], ry_send.at[slot, step], ry_recv.at[slot, step],
                    "tensor", (t + step) % T,
                ),
                cond, row_sent,
            )

    def row_c(slot, tstep, cond):
        block = ((t + T - tstep) % T) * C + c
        for step in range(1, C):
            send(
                lambda step=step: remote(
                    rows.at[block, slot], rows.at[block, slot],
                    rc_send.at[slot, tstep, step], rc_recv.at[slot, tstep, step],
                    "dp", (c + step) % C,
                ),
                cond, row_sent,
            )

    def row_step(step):
        for (slot, cond), move in zip(near(step), (1, -1)):
            when(cond, lambda slot=slot: row_wait_z(slot))
            more = (a + 1 < R) if move > 0 else (a > 0)
            row_z(slot, move, both(cond, more))
            row_y(slot, cond)
            row_c(slot, 0, cond)

    row_z(a, 1, a + 1 < R)
    row_z(a, -1, a > 0)
    row_y(a, True)
    row_c(a, 0, True)
    for m in range(1, p.mats):
        send_x(m, a, True, own=True)

    fresh_ids = lax.broadcasted_iota(jnp.int32, (p.rows, p.rows), 1)
    filler = (fresh_ids == fill_col[...]).astype(jnp.bfloat16)
    out[...] = jnp.dot(filler, fresh[...], preferred_element_type=jnp.float32).astype(jnp.bfloat16)

    if R > 1:
        row_step(1)
    send_z(1)
    forward_z(0, near(1) if R > 1 else [])
    for step in range(2, R):
        row_step(step)
        forward_z(0, near(step))
    for h in range(p.halves):
        send_z(2 + h)
    for slot, cond in by_distance:
        for tstep in range(1, T):
            place = lambda: rows.at[((t + T - tstep) % T) * C + c, slot]
            when(
                cond,
                lambda: remote(
                    place(), place(), ry_send.at[slot, tstep], ry_recv.at[slot, tstep],
                    "tensor", (t + T - tstep) % T,
                ).wait_recv(),
            )
            row_c(slot, tstep, cond)
    for slot in range(R):
        for tstep in range(T):
            for step in range(1, C):
                place = rows.at[((t + T - tstep) % T) * C + (c + C - step) % C, slot]
                remote(
                    place, place, rc_send.at[slot, tstep, step], rc_recv.at[slot, tstep, step],
                    "dp", (c + C - step) % C,
                ).wait_recv()

    per_owner = S // p.unit
    for m in range(p.mats):
        local(m).wait()

    def product_block(block, weights, acc, first):
        span = pl.ds(pl.multiple_of(block * width, width), width)

        def body(slot, carry):
            part = jnp.dot(rows[block, slot], weights[span, :], preferred_element_type=jnp.float32)
            acc[slot] = part if first else acc[slot] + part
            return carry

        lax.fori_loop(0, R, body, 0)

    def products(m, weights, acc, pairs):
        for frm, cond in pairs:
            def run(frm=frm, first=cond is True):
                for step in range(1, S):
                    wait_x(m, frm, step)
                for k in range(per_owner):
                    product_block(frm * per_owner + k, weights, acc, first and k == 0)
            when(cond, run)

    products(0, gate_full, gate_acc, by_distance)
    products(1, up_full, up_acc, by_distance[:1])
    for step in range(1, R):
        forward_z(1, near(step))
        if step > 1:
            products(1, up_full, up_acc, near(step - 1))
    if R > 1:
        products(1, up_full, up_acc, near(R - 1))

    def activate(slot, carry):
        gate = gate_acc[slot]
        hidden[slot] = (gate / (1.0 + jnp.exp(-gate)) * up_acc[slot]).astype(jnp.bfloat16)
        return carry

    lax.fori_loop(0, R, activate, 0)
    for make, cond in row_sent:
        when(cond, lambda make=make: make().wait_send())

    def slot_at(index):
        return jnp.where(index % 2 == 0, R - 1 - index // 2, index // 2)

    def column_part(n):
        return n // p.unit, (b + n % p.unit) % p.unit

    def product(n, slot, block):
        h, i = column_part(n)
        return jnp.dot(hidden[slot], down_full[h, block * p.unit + i], preferred_element_type=jnp.float32)

    def stage(n, block, slot):
        return rows.at[block, slot, :, n * pw : (n + 1) * pw]

    def out_c(n, tstep, slot, step):
        return remote(
            stage(n, tstep * (C - 1) + step - 1, slot), crecv.at[n, tstep, slot, step - 1],
            oc_send.at[n, tstep, slot, step - 1], oc_recv.at[n, tstep, slot, step - 1],
            "dp", (c + step) % C,
        )

    def out_y(n, tstep, slot):
        return remote(
            stage(n, T * (C - 1) + tstep, slot), yrecv.at[n, tstep, slot],
            oy_send.at[n, tstep, slot], oy_recv.at[n, tstep, slot],
            "tensor", (t + 1 + tstep) % T,
        )

    def out_z(n, slot):
        to = jnp.where(slot > a, a + 1, a - 1)
        land = jnp.where(slot == a - 1, R, slot)
        return remote(
            stage(n, K - 1, slot), zrecv.at[n, land], oz_send.at[n, slot], oz_recv.at[n, land],
            "fsdp", to * S + b,
        )

    def wait_out_z(n, land):
        place = zrecv.at[n, land]
        remote(place, place, oz_send.at[n, 0], oz_recv.at[n, land], "fsdp", ((a + 1) % R) * S + b).wait_recv()

    def part_a(n):
        h, turn = n // p.unit, n % p.unit
        m = 2 + h
        if turn == 0:
            forward_z(m, arrivals)
        for frm in range(R):
            for step in range(1, S):
                if (step + turn) % p.unit == 0:
                    wait_x(m, frm, step)

        def body(index, carry):
            tstep, slot = index // R, slot_at(index % R)
            for step in range(1, C):
                block = ((t + 1 + tstep) % T) * C + (c + step) % C
                place = stage(n, tstep * (C - 1) + step - 1, slot)
                place[...] = product(n, slot, block).astype(jnp.bfloat16)
                out_c(n, tstep, slot, step).start()
            return carry

        lax.fori_loop(0, T * R, body, 0)

    def chip_sum(n, tstep, slot):
        value = product(n, slot, ((t + 1 + tstep) % T) * C + c)
        for step in range(1, C):
            out_c(n, tstep, slot, step).wait_recv()
            value = value + crecv[n, tstep, slot, step - 1].astype(jnp.float32)
        return value

    def part_b(n):
        def body(index, carry):
            tstep, slot = index // R, slot_at(index % R)
            place = stage(n, T * (C - 1) + tstep, slot)
            place[...] = chip_sum(n, tstep, slot).astype(jnp.bfloat16)
            out_y(n, tstep, slot).start()
            return carry

        lax.fori_loop(0, (T - 1) * R, body, 0)

    def pass_on(n, slot, value):
        place = stage(n, K - 1, slot)
        place[...] = value.astype(jnp.bfloat16)
        out_z(n, slot).start()

    def part_c(n):
        def body(index, carry):
            slot = slot_at(index)
            value = chip_sum(n, T - 1, slot)
            for tstep in range(T - 1):
                out_y(n, tstep, slot).wait_recv()
                value = value + yrecv[n, tstep, slot].astype(jnp.float32)
            mine[n, slot] = value
            head = jnp.logical_or(
                jnp.logical_and(a == 0, slot > a), jnp.logical_and(a == R - 1, slot < a)
            )
            pl.when(head)(lambda: pass_on(n, slot, mine[n, slot]))
            return carry

        lax.fori_loop(0, R, body, 0)

    def part_d(n):
        def body(index, carry):
            slot = slot_at(index)
            middle = jnp.logical_or(
                jnp.logical_and(slot > a, a > 0), jnp.logical_and(slot < a, a < R - 1)
            )

            @pl.when(middle)
            def _():
                wait_out_z(n, slot)
                pass_on(n, slot, mine[n, slot] + zrecv[n, slot].astype(jnp.float32))

            return carry

        lax.fori_loop(0, R, body, 0)
        for cond, land in ((a > 0, a), (a < R - 1, R)):
            @pl.when(cond)
            def _():
                wait_out_z(n, land)
                mine[n, a] = mine[n, a] + zrecv[n, land].astype(jnp.float32)

        h, i = column_part(n)
        columns = pl.ds(pl.multiple_of(i * fw + h * pw, pw), pw)
        settled = (kept[:, columns].astype(jnp.float32) + mine[n, a]).astype(jnp.bfloat16)
        slots = lax.broadcasted_iota(jnp.int32, (p.rows, cap), 1)
        spread = (slots == pick_col[...]).astype(jnp.bfloat16)
        placed = jnp.dot(spread, settled, preferred_element_type=jnp.float32)
        out[:, columns] = (placed + out[:, columns].astype(jnp.float32)).astype(jnp.bfloat16)

    for n in range(p.parts + 2):
        if n < p.parts:
            part_a(n)
            part_b(n)
        if 1 <= n <= p.parts:
            part_c(n - 1)
        if n >= 2:
            part_d(n - 2)

    for make, cond in sent:
        when(cond, lambda make=make: make().wait_send())

    def settle(index, carry):
        n, slot = index // R, index % R
        for tstep in range(T):
            for step in range(1, C):
                place = crecv.at[n, tstep, slot, step - 1]
                remote(
                    place, place, oc_send.at[n, tstep, slot, step - 1],
                    oc_recv.at[n, tstep, slot, step - 1], "dp", (c + step) % C,
                ).wait_send()
        for tstep in range(T - 1):
            place = yrecv.at[n, tstep, slot]
            remote(
                place, place, oy_send.at[n, tstep, slot], oy_recv.at[n, tstep, slot],
                "tensor", (t + 1 + tstep) % T,
            ).wait_send()

        @pl.when(slot != a)
        def _():
            place = zrecv.at[n, slot]
            remote(
                place, place, oz_send.at[n, slot], oz_recv.at[n, slot],
                "fsdp", ((a + 1) % R) * S + b,
            ).wait_send()

        return carry

    lax.fori_loop(0, p.parts * R, settle, 0)


def make_body(mesh):
    def body(states, fresh_rows, norm_gain, gate_weight, up_weight, down_weight, halted, refill_index):
        p = Plan(mesh, states, gate_weight, down_weight)
        R, S, T, C, K = p.R, p.S, p.T, p.C, p.K
        cap, width, fw, hp, pw = p.cap, p.width, p.fw, p.hp, p.pw
        running = halted.reshape(p.rows) == 0
        slot_of = jnp.cumsum(running.astype(jnp.int32)) - 1
        pick = jnp.where(running, slot_of, -1)
        blocks, batch = refill_index.shape
        base = lax.broadcasted_iota(jnp.int32, (blocks, batch), 0) * batch
        fill = jnp.where(running, -1, (base + refill_index).reshape(p.rows))
        bf16, f32 = jnp.bfloat16, jnp.float32
        dma = lambda *shape: pltpu.SemaphoreType.DMA(shape)
        vmem = pl.BlockSpec(memory_space=pltpu.VMEM)
        hbm = pl.BlockSpec(memory_space=pl.ANY)
        return pl.pallas_call(
            functools.partial(block_kernel, p),
            out_shape=jax.ShapeDtypeStruct(states.shape, states.dtype),
            in_specs=[vmem] * 6 + [hbm] * 3,
            out_specs=vmem,
            scratch_shapes=[
                pltpu.VMEM((K, R, cap, width), bf16),
                pltpu.VMEM((p.features, hp), bf16),
                pltpu.VMEM((p.features, hp), bf16),
                pltpu.VMEM((p.halves, p.F, hp, pw), bf16),
                pltpu.VMEM((R, cap, hp), f32),
                pltpu.VMEM((R, cap, hp), f32),
                pltpu.VMEM((R, cap, hp), bf16),
                pltpu.VMEM((cap, width), bf16),
                pltpu.VMEM((C, cap, 128), f32),
                pltpu.VMEM((T, cap, 128), f32),
                pltpu.VMEM((p.parts, T, R, max(1, C - 1), cap, pw), bf16),
                pltpu.VMEM((p.parts, max(1, T - 1), R, cap, pw), bf16),
                pltpu.VMEM((p.parts, R + 1, cap, pw), bf16),
                pltpu.VMEM((p.parts, R, cap, pw), f32),
                dma(p.mats),
                dma(p.mats, R), dma(p.mats, R),
                dma(p.mats, R, S), dma(p.mats, R, S),
                dma(2, R), dma(R),
                dma(R, T), dma(R, T),
                dma(R, T, C), dma(R, T, C),
                dma(C), dma(C), dma(T), dma(T),
                dma(p.parts, T, R, max(1, C - 1)), dma(p.parts, T, R, max(1, C - 1)),
                dma(p.parts, max(1, T - 1), R), dma(p.parts, max(1, T - 1), R),
                dma(p.parts, R), dma(p.parts, R + 1),
            ],
            compiler_params=pltpu.CompilerParams(
                collective_id=0, has_side_effects=True, vmem_limit_bytes=64000 * 1024
            ),
        )(
            pick.reshape(1, p.rows), pick.reshape(p.rows, 1), fill.reshape(p.rows, 1),
            states, fresh_rows, norm_gain.reshape(1, width), gate_weight, up_weight, down_weight,
        )

    return body


def solution(mesh):
    columns = ("tensor", "dp")
    in_specs = (
        P("fsdp", columns),
        P("fsdp", columns),
        P(columns),
        P("fsdp", columns),
        P("fsdp", columns),
        P(columns, "fsdp"),
        P("fsdp", None),
        P("fsdp", None),
    )
    return jax.shard_map(
        make_body(mesh), mesh=mesh, in_specs=in_specs, out_specs=P("fsdp", columns), check_vma=False
    )
```

profile of v0, /device:TPU:8, one launch (start us, length us, event | category | flops | bytes accessed | tf_op | source)
XLA Modules:
  0.0 333.0 jit_solution(15668403452957107039)
XLA Ops:
  0.0 0.8 broadcast_add_fusion
  0.8 1.3 reshape.119.gain
  2.0 0.7 fusion
  2.7 0.1 reshape.120
  2.8 0.3 reduce-window.9
  3.1 0.1 slice.7
  3.2 0.1 slice_reduce_fusion
  3.3 0.1 add_add_fusion
  3.4 0.1 eq.34
  3.5 0.6 broadcast_select_fusion.2.pick_row
  4.1 0.3 eq.36
  4.4 0.2 reshape.121
  4.6 0.1 copy.10
  4.7 0.9 broadcast_select_fusion
  5.6 325.2 %shard_map.82 = bf16[512,1024]{1,0:T(8,128)(2,1)} custom-call(s32[1,512]{1,0:T(1,128)} %broadcast_select_fusion.2.pick_row, s32[512,1]{1,0:T(8,128)} %get-tuple-element.8.pick_col, s32[512,1]{1,0:T(8,128)} %get-tuple-element.7.fill_col, bf16[512,1024]{1,0:T(8,128)(2,1)} %states.1, bf16[512,1024]{1,0:T(8,128)(2,1)} %fresh.1, bf16[1,1024]{1,0:T(2,128)(2,1)} %reshape.119.gain, ...), custom_call_target="tpu_custom_call" | custom-call | tf_op jit(solution)/shard_map/pallas_call | solution.py:479
  330.8 2.3 copy.14
  (2 shorter events, 0.0 us)
where the time goes:
time: 338 us; the launch traced here: 333 us
  Pallas kernels  325 us (96%)
  local copies, waits for them, and re-layouts  4.49 us (1%)
    pallas_call x1, Pallas kernels, body(): pl.pallas_call(functools.partial(block_kernel, p), out_shape=jax.ShapeDty...  325 us

commit v1 on v0

--- a/solution.py
+++ b/solution.py
@@ -83,9 +83,12 @@
             return (gate_full, up_full)[m].at[pl.ds(pl.multiple_of(owner * fw, fw), fw), :]
         return down_full.at[m - 2, owner]
 
-    def send_z(m):
-        for step in range(R - 1, 0, -1):
+    at_end = jnp.logical_or(a == 0, a == R - 1)
+
+    def send_z(m, steps, where=None):
+        for step in steps:
             for to, cond in near(step):
+                cond = cond if where is None else jnp.logical_and(cond, where)
                 send(
                     lambda m=m, to=to: remote(
                         source_at(m, to), full_at(m, f), gz_send.at[m, to], gz_recv.at[m, a],
@@ -133,7 +136,9 @@
         pl.semaphore_signal(barrier, inc=1, device_id={axis: index}, device_id_type=MESH)
     pl.semaphore_wait(barrier, len(partners))
 
-    send_z(0)
+    far = list(range(2, R))
+    close = range(1, min(R, 2))
+    send_z(0, close)
     send_x(0, a, True, own=True)
     for m in range(p.mats):
         local(m).start()
@@ -214,6 +219,7 @@
 
     row_z(a, 1, a + 1 < R)
     row_z(a, -1, a > 0)
+    send_z(1, close, at_end)
     row_y(a, True)
     row_c(a, 0, True)
     for m in range(1, p.mats):
@@ -223,26 +229,54 @@
     filler = (fresh_ids == fill_col[...]).astype(jnp.bfloat16)
     out[...] = jnp.dot(filler, fresh[...], preferred_element_type=jnp.float32).astype(jnp.bfloat16)
 
-    if R > 1:
-        row_step(1)
-    send_z(1)
-    forward_z(0, near(1) if R > 1 else [])
-    for step in range(2, R):
+    def row_arrive_y(pairs):
+        for slot, cond in pairs:
+            for tstep in range(1, T):
+                place = lambda: rows.at[((t + T - tstep) % T) * C + c, slot]
+                when(
+                    cond,
+                    lambda: remote(
+                        place(), place(), ry_send.at[slot, tstep], ry_recv.at[slot, tstep],
+                        "tensor", (t + T - tstep) % T,
+                    ).wait_recv(),
+                )
+                row_c(slot, tstep, cond)
+
+    inner = jnp.logical_not(at_end)
+    beyond = range(3, R)
+
+    def only(pairs, where):
+        return [(frm, both(cond, where)) for frm, cond in pairs]
+
+    def rim(pairs, yes):
+        picked = []
+        for frm, cond in pairs:
+            end = jnp.logical_or(frm == 0, frm == R - 1)
+            picked.append((frm, both(cond, end if yes else jnp.logical_not(end))))
+        return picked
+
+    for step in range(1, min(R, 3)):
         row_step(step)
+        if step == 1:
+            forward_z(0, near(1))
+    send_z(1, close, inner)
+    send_z(0, far, inner)
+    send_z(1, far, inner)
+    for step in beyond:
+        row_step(step)
+    send_z(0, far[::-1], at_end)
+    send_z(1, far[::-1], at_end)
+    for h in range(p.halves):
+        send_z(2 + h, close, at_end)
+    send_z(2, far, at_end)
+    row_arrive_y(by_distance[:3])
+    forward_z(0, only(near(2), at_end))
+    forward_z(1, only(near(2), at_end))
+    forward_z(1, near(1))
+    row_arrive_y(by_distance[3:])
+    forward_z(0, only(near(2), inner))
+    for step in beyond:
         forward_z(0, near(step))
-    for h in range(p.halves):
-        send_z(2 + h)
-    for slot, cond in by_distance:
-        for tstep in range(1, T):
-            place = lambda: rows.at[((t + T - tstep) % T) * C + c, slot]
-            when(
-                cond,
-                lambda: remote(
-                    place(), place(), ry_send.at[slot, tstep], ry_recv.at[slot, tstep],
-                    "tensor", (t + T - tstep) % T,
-                ).wait_recv(),
-            )
-            row_c(slot, tstep, cond)
     for slot in range(R):
         for tstep in range(T):
             for step in range(1, C):
@@ -251,6 +285,9 @@
                     place, place, rc_send.at[slot, tstep, step], rc_recv.at[slot, tstep, step],
                     "dp", (c + C - step) % C,
                 ).wait_recv()
+    for h in range(p.halves):
+        send_z(2 + h, close, inner)
+        send_z(2 + h, far, inner)
 
     per_owner = S // p.unit
     for m in range(p.mats):
@@ -266,7 +303,8 @@
 
         lax.fori_loop(0, R, body, 0)
 
-    def products(m, weights, acc, pairs):
+    def products(m, pairs):
+        weights, acc = ((gate_full, gate_acc), (up_full, up_acc))[m]
         for frm, cond in pairs:
             def run(frm=frm, first=cond is True):
                 for step in range(1, S):
@@ -275,14 +313,18 @@
                     product_block(frm * per_owner + k, weights, acc, first and k == 0)
             when(cond, run)
 
-    products(0, gate_full, gate_acc, by_distance)
-    products(1, up_full, up_acc, by_distance[:1])
+    products(0, by_distance[:1])
     for step in range(1, R):
+        products(0, near(step))
+    products(1, by_distance[:1])
+    products(1, near(1))
+    products(1, only(near(2), at_end))
+    forward_z(1, only(near(2), inner))
+    products(1, only(near(2), inner))
+    for step in beyond:
         forward_z(1, near(step))
-        if step > 1:
-            products(1, up_full, up_acc, near(step - 1))
-    if R > 1:
-        products(1, up_full, up_acc, near(R - 1))
+    for step in beyond:
+        products(1, near(step))
 
     def activate(slot, carry):
         gate = gate_acc[slot]
@@ -337,6 +379,8 @@
         m = 2 + h
         if turn == 0:
             forward_z(m, arrivals)
+            if h + 1 < p.halves:
+                send_z(m + 1, far, at_end)
         for frm in range(R):
             for step in range(1, S):
                 if (step + turn) % p.unit == 0:
@@ -360,22 +404,23 @@
             value = value + crecv[n, tstep, slot, step - 1].astype(jnp.float32)
         return value
 
-    def part_b(n):
+    def part_b(n, low, high):
         def body(index, carry):
-            tstep, slot = index // R, slot_at(index % R)
+            tstep, slot = index // (high - low), slot_at(low + index % (high - low))
             place = stage(n, T * (C - 1) + tstep, slot)
             place[...] = chip_sum(n, tstep, slot).astype(jnp.bfloat16)
             out_y(n, tstep, slot).start()
             return carry
 
-        lax.fori_loop(0, (T - 1) * R, body, 0)
+        if high > low:
+            lax.fori_loop(0, (T - 1) * (high - low), body, 0)
 
     def pass_on(n, slot, value):
         place = stage(n, K - 1, slot)
         place[...] = value.astype(jnp.bfloat16)
         out_z(n, slot).start()
 
-    def part_c(n):
+    def part_c(n, low, high):
         def body(index, carry):
             slot = slot_at(index)
             value = chip_sum(n, T - 1, slot)
@@ -389,23 +434,24 @@
             pl.when(head)(lambda: pass_on(n, slot, mine[n, slot]))
             return carry
 
-        lax.fori_loop(0, R, body, 0)
-
-    def part_d(n):
+        lax.fori_loop(low, high, body, 0)
+
+    def part_s(n, low, high, hop):
         def body(index, carry):
             slot = slot_at(index)
-            middle = jnp.logical_or(
-                jnp.logical_and(slot > a, a > 0), jnp.logical_and(slot < a, a < R - 1)
-            )
-
-            @pl.when(middle)
+            up = jnp.logical_and(a == hop, slot > a)
+            down = jnp.logical_and(a == R - 1 - hop, slot < a)
+
+            @pl.when(jnp.logical_or(up, down))
             def _():
                 wait_out_z(n, slot)
                 pass_on(n, slot, mine[n, slot] + zrecv[n, slot].astype(jnp.float32))
 
             return carry
 
-        lax.fori_loop(0, R, body, 0)
+        lax.fori_loop(low, high, body, 0)
+
+    def part_f(n):
         for cond, land in ((a > 0, a), (a < R - 1, R)):
             @pl.when(cond)
             def _():
@@ -420,14 +466,32 @@
         placed = jnp.dot(spread, settled, preferred_element_type=jnp.float32)
         out[:, columns] = (placed + out[:, columns].astype(jnp.float32)).astype(jnp.bfloat16)
 
-    for n in range(p.parts + 2):
-        if n < p.parts:
-            part_a(n)
-            part_b(n)
-        if 1 <= n <= p.parts:
-            part_c(n - 1)
-        if n >= 2:
-            part_d(n - 2)
+    edge = min(2, R)
+    groups = [(0, edge)] + ([(edge, R)] if R > edge else [])
+    steady = max(0, p.parts - 2)
+    units = [(n, *group) for n in range(steady) for group in groups]
+    units += [(n, *group) for group in groups for n in range(steady, p.parts)]
+    first = len(groups)
+    for n in range(p.parts):
+        part_a(n)
+        part_b(n, 0, R if n < steady else edge)
+        if n == 1:
+            for unit in units[:first]:
+                part_c(*unit)
+    for n in range(steady, p.parts):
+        part_b(n, edge, R)
+    closed = {}
+    for index, unit in enumerate(units):
+        closed[unit[0]] = index + R - 2
+    for index in range(len(units) + R - 2):
+        if index < len(units) and (index >= first or p.parts < 2):
+            part_c(*units[index])
+        for hop in range(1, R - 1):
+            if 0 <= index + 1 - hop < len(units):
+                part_s(*units[index + 1 - hop], hop)
+        for n in range(p.parts):
+            if closed[n] == index:
+                part_f(n)
 
     for make, cond in sent:
         when(cond, lambda make=make: make().wait_send())

time: 338 us -> 268 us (0.79); the launches traced: 333 us -> 267 us
  Pallas kernels: 325 us -> 260 us
    pallas_call x1, Pallas kernels: 325 us -> 260 us  [body(): pl.pallas_call(functools.partial(block_kernel, p), out_shape=jax.ShapeDty...]
where the time goes in v1:
time: 268 us; the launch traced here: 267 us
  Pallas kernels  260 us (97%)
  local copies, waits for them, and re-layouts  4.49 us (2%)
  other arithmetic  3.31 us (1%)
    pallas_call x1, Pallas kernels, body(): pl.pallas_call(functools.partial(block_kernel, p), out_shape=jax.ShapeDty...  260 us

profile of v1, /device:TPU:8, one launch (start us, length us, event | category | flops | bytes accessed | tf_op | source)
XLA Modules:
  0.0 267.4 jit_solution(5976330657024964539)
XLA Ops:
  0.0 0.8 broadcast_add_fusion
  0.8 1.3 reshape.119.gain
  2.0 0.7 fusion
  2.7 0.1 reshape.120
  2.8 0.3 reduce-window.9
  3.1 0.1 slice.7
  3.2 0.1 slice_reduce_fusion
  3.3 0.1 add_add_fusion
  3.4 0.1 eq.34
  3.5 0.6 broadcast_select_fusion.2.pick_row
  4.1 0.3 eq.36
  4.4 0.2 reshape.121
  4.6 0.1 copy.10
  4.7 0.9 broadcast_select_fusion
  5.6 259.6 %shard_map.82 = bf16[512,1024]{1,0:T(8,128)(2,1)} custom-call(s32[1,512]{1,0:T(1,128)} %broadcast_select_fusion.2.pick_row, s32[512,1]{1,0:T(8,128)} %get-tuple-element.8.pick_col, s32[512,1]{1,0:T(8,128)} %get-tuple-element.7.fill_col, bf16[512,1024]{1,0:T(8,128)(2,1)} %states.1, bf16[512,1024]{1,0:T(8,128)(2,1)} %fresh.1, bf16[1,1024]{1,0:T(2,128)(2,1)} %reshape.119.gain, ...), custom_call_target="tpu_custom_call" | custom-call | tf_op jit(solution)/shard_map/pallas_call | solution.py:543
  265.1 2.3 copy.14
  (2 shorter events, 0.0 us)

commit v2 on v1

--- a/solution.py
+++ b/solution.py
@@ -23,7 +23,7 @@
         self.features = self.width * self.K
         self.fw = gate.shape[0]
         self.hp = gate.shape[1] // self.R
-        self.halves = 2 if self.fw % 256 == 0 else 1
+        self.halves = self.fw // 128
         self.pw = self.fw // self.halves
         self.mats = 2 + self.halves
         self.parts = self.unit * self.halves
@@ -37,7 +37,7 @@
     crecv, yrecv, zrecv, mine,
     local_sem, gz_send, gz_recv, xs_send, xs_recv, rz_send, rz_recv, ry_send, ry_recv,
     rc_send, rc_recv, mc_send, mc_recv, mt_send, mt_recv,
-    oc_send, oc_recv, oy_send, oy_recv, oz_send, oz_recv,
+    oc_send, oc_recv, oy_send, oy_recv, oz_send, oz_recv, pair_sem,
 ):
     R, S, T, C, K = p.R, p.S, p.T, p.C, p.K
     cap, width, fw, hp, pw = p.cap, p.width, p.fw, p.hp, p.pw
@@ -85,10 +85,11 @@
 
     at_end = jnp.logical_or(a == 0, a == R - 1)
 
-    def send_z(m, steps, where=None):
+    def send_z(m, steps, where=None, choose=None):
         for step in steps:
             for to, cond in near(step):
                 cond = cond if where is None else jnp.logical_and(cond, where)
+                cond = cond if choose is None else jnp.logical_and(cond, choose(to))
                 send(
                     lambda m=m, to=to: remote(
                         source_at(m, to), full_at(m, f), gz_send.at[m, to], gz_recv.at[m, a],
@@ -259,24 +260,35 @@
         row_step(step)
         if step == 1:
             forward_z(0, near(1))
-    send_z(1, close, inner)
+    send_z(1, close, inner, lambda to: jnp.logical_and(to > 0, to < R - 1))
     send_z(0, far, inner)
     send_z(1, far, inner)
+    forward_z(0, only(near(2), at_end))
+    forward_z(1, only(near(2), at_end))
+    if C > 1:
+        @pl.when(at_end)
+        def _():
+            for step in range(1, C):
+                pl.semaphore_signal(
+                    pair_sem, inc=1, device_id={"dp": (c + step) % C}, device_id_type=MESH
+                )
+            pl.semaphore_wait(pair_sem, C - 1)
+
+    for m in range(2):
+        send_z(m, far[:1], at_end)
     for step in beyond:
         row_step(step)
-    send_z(0, far[::-1], at_end)
-    send_z(1, far[::-1], at_end)
+    for m in range(2):
+        send_z(m, beyond, at_end)
     for h in range(p.halves):
         send_z(2 + h, close, at_end)
     send_z(2, far, at_end)
     row_arrive_y(by_distance[:3])
-    forward_z(0, only(near(2), at_end))
-    forward_z(1, only(near(2), at_end))
-    forward_z(1, near(1))
+    forward_z(1, only(near(1), inner))
     row_arrive_y(by_distance[3:])
+    send_z(1, close, inner, lambda to: jnp.logical_or(to == 0, to == R - 1))
+    forward_z(1, only(near(1), at_end))
     forward_z(0, only(near(2), inner))
-    for step in beyond:
-        forward_z(0, near(step))
     for slot in range(R):
         for tstep in range(T):
             for step in range(1, C):
@@ -314,15 +326,19 @@
             when(cond, run)
 
     products(0, by_distance[:1])
-    for step in range(1, R):
-        products(0, near(step))
+    products(0, near(1))
+    forward_z(1, only(near(2), inner))
+    products(0, only(near(2), at_end))
+    for step in beyond:
+        forward_z(0, near(step))
     products(1, by_distance[:1])
+    products(1, only(near(2), at_end))
     products(1, near(1))
-    products(1, only(near(2), at_end))
-    forward_z(1, only(near(2), inner))
-    products(1, only(near(2), inner))
     for step in beyond:
         forward_z(1, near(step))
+        products(0, near(step))
+    products(0, only(near(2), inner))
+    products(1, only(near(2), inner))
     for step in beyond:
         products(1, near(step))
 
@@ -466,32 +482,18 @@
         placed = jnp.dot(spread, settled, preferred_element_type=jnp.float32)
         out[:, columns] = (placed + out[:, columns].astype(jnp.float32)).astype(jnp.bfloat16)
 
-    edge = min(2, R)
-    groups = [(0, edge)] + ([(edge, R)] if R > edge else [])
-    steady = max(0, p.parts - 2)
-    units = [(n, *group) for n in range(steady) for group in groups]
-    units += [(n, *group) for group in groups for n in range(steady, p.parts)]
-    first = len(groups)
-    for n in range(p.parts):
-        part_a(n)
-        part_b(n, 0, R if n < steady else edge)
-        if n == 1:
-            for unit in units[:first]:
-                part_c(*unit)
-    for n in range(steady, p.parts):
-        part_b(n, edge, R)
-    closed = {}
-    for index, unit in enumerate(units):
-        closed[unit[0]] = index + R - 2
-    for index in range(len(units) + R - 2):
-        if index < len(units) and (index >= first or p.parts < 2):
-            part_c(*units[index])
+    behind = 2
+    for tick in range(p.parts + behind + R - 1):
+        if tick < p.parts:
+            part_a(tick)
+            part_b(tick, 0, R)
+        if 0 <= tick - behind < p.parts:
+            part_c(tick - behind, 0, R)
         for hop in range(1, R - 1):
-            if 0 <= index + 1 - hop < len(units):
-                part_s(*units[index + 1 - hop], hop)
-        for n in range(p.parts):
-            if closed[n] == index:
-                part_f(n)
+            if 0 <= tick - behind + 1 - hop < p.parts:
+                part_s(tick - behind + 1 - hop, 0, R, hop)
+        if 0 <= tick - behind - R + 2 < p.parts:
+            part_f(tick - behind - R + 2)
 
     for make, cond in sent:
         when(cond, lambda make=make: make().wait_send())
@@ -570,6 +572,7 @@
                 dma(p.parts, T, R, max(1, C - 1)), dma(p.parts, T, R, max(1, C - 1)),
                 dma(p.parts, max(1, T - 1), R), dma(p.parts, max(1, T - 1), R),
                 dma(p.parts, R), dma(p.parts, R + 1),
+                pltpu.SemaphoreType.REGULAR,
             ],
             compiler_params=pltpu.CompilerParams(
                 collective_id=0, has_side_effects=True, vmem_limit_bytes=64000 * 1024

time: 268 us -> 256 us (0.955); the launches traced: 267 us -> 252 us
  Pallas kernels: 260 us -> 244 us
    pallas_call x1, Pallas kernels: 260 us -> 244 us  [body(): pl.pallas_call(functools.partial(block_kernel, p), out_shape=jax.ShapeDty...]
where the time goes in v2:
time: 256 us; the launch traced here: 252 us
  Pallas kernels  244 us (95%)
  local copies, waits for them, and re-layouts  4.49 us (2%)
  other arithmetic  3.31 us (1%)
    pallas_call x1, Pallas kernels, body(): pl.pallas_call(functools.partial(block_kernel, p), out_shape=jax.ShapeDty...  244 us

profile of v2, /device:TPU:8, one launch (start us, length us, event | category | flops | bytes accessed | tf_op | source)
XLA Modules:
  0.0 251.9 jit_solution(1052270910233188011)
XLA Ops:
  0.0 0.8 broadcast_add_fusion
  0.8 1.3 reshape.119.gain
  2.0 0.7 fusion
  2.7 0.1 reshape.120
  2.8 0.3 reduce-window.9
  3.1 0.1 slice.7
  3.2 0.1 slice_reduce_fusion
  3.3 0.1 add_add_fusion
  3.4 0.1 eq.34
  3.5 0.6 broadcast_select_fusion.2.pick_row
  4.1 0.3 eq.36
  4.4 0.2 reshape.121
  4.6 0.1 copy.10
  4.7 0.9 broadcast_select_fusion
  5.6 244.1 %shard_map.82 = bf16[512,1024]{1,0:T(8,128)(2,1)} custom-call(s32[1,512]{1,0:T(1,128)} %broadcast_select_fusion.2.pick_row, s32[512,1]{1,0:T(8,128)} %get-tuple-element.8.pick_col, s32[512,1]{1,0:T(8,128)} %get-tuple-element.7.fill_col, bf16[512,1024]{1,0:T(8,128)(2,1)} %states.1, bf16[512,1024]{1,0:T(8,128)(2,1)} %fresh.1, bf16[1,1024]{1,0:T(2,128)(2,1)} %reshape.119.gain, ...), custom_call_target="tpu_custom_call" | custom-call | tf_op jit(solution)/shard_map/pallas_call | solution.py:545
  249.7 2.3 copy.14
  (2 shorter events, 0.0 us)

commit v3 on v2

--- a/solution.py
+++ b/solution.py
@@ -31,13 +31,14 @@
 
 def block_kernel(
     p,
-    pick_row, pick_col, fill_col, states, fresh, gain, gate_w, up_w, down_w,
-    out,
+    halted, refill, gain, states_in, fresh_in, gate_w, up_w, down_w,
+    result,
+    states, fresh, out, picker, spread,
     rows, gate_full, up_full, down_full, gate_acc, up_acc, hidden, kept, ms_c, ms_t,
     crecv, yrecv, zrecv, mine,
     local_sem, gz_send, gz_recv, xs_send, xs_recv, rz_send, rz_recv, ry_send, ry_recv,
     rc_send, rc_recv, mc_send, mc_recv, mt_send, mt_recv,
-    oc_send, oc_recv, oy_send, oy_recv, oz_send, oz_recv, pair_sem,
+    oc_send, oc_recv, oy_send, oy_recv, oz_send, oz_recv, pair_sem, in_sem, out_sem,
 ):
     R, S, T, C, K = p.R, p.S, p.T, p.C, p.K
     cap, width, fw, hp, pw = p.cap, p.width, p.fw, p.hp, p.pw
@@ -128,6 +129,12 @@
             when(cond, lambda frm=frm: wait_z(m, frm))
             send_x(m, frm, cond)
 
+    fetch = [
+        pltpu.make_async_copy(source, place, in_sem.at[k])
+        for k, (source, place) in enumerate(((states_in, states), (fresh_in, fresh)))
+    ]
+    for copy in fetch:
+        copy.start()
     barrier = pltpu.get_barrier_semaphore()
     partners = [("fsdp", ((a + step) % R) * S + b) for step in range(1, R)]
     partners += [("fsdp", a * S + (b + step) % S) for step in range(1, S)]
@@ -144,9 +151,26 @@
     for m in range(p.mats):
         local(m).start()
 
-    ids = lax.broadcasted_iota(jnp.int32, (cap, p.rows), 0)
-    picker = (ids == pick_row[...]).astype(jnp.bfloat16)
-    picked = jnp.dot(picker, states[...], preferred_element_type=jnp.float32)
+    blocks, batch = halted.shape
+    f32, bf16, i32 = jnp.float32, jnp.bfloat16, jnp.int32
+
+    def ids(shape, axis):
+        return lax.broadcasted_iota(i32, shape, axis)
+
+    within = lax.rem(ids((batch, p.rows), 1), batch) == ids((batch, p.rows), 0)
+    block_of = lax.div(ids((blocks, p.rows), 1), batch) == ids((blocks, p.rows), 0)
+
+    def flat(table):
+        wide = jnp.dot(table.astype(f32).astype(bf16), within.astype(bf16), preferred_element_type=f32)
+        return jnp.sum(jnp.where(block_of, wide, 0.0), axis=0, keepdims=True)
+
+    running = flat((halted[...] == 0).astype(i32))
+    upto = (ids((p.rows, p.rows), 0) <= ids((p.rows, p.rows), 1)).astype(bf16)
+    count = jnp.dot(jnp.broadcast_to(running, (8, p.rows)).astype(bf16), upto, preferred_element_type=f32)
+    slot_row = jnp.where(running > 0.5, count[:1] - 1.0, -1.0).astype(i32)
+    picker[...] = (ids((cap, p.rows), 0) == slot_row).astype(bf16)
+    fetch[0].wait()
+    picked = jnp.dot(picker[...], states[...], preferred_element_type=f32)
     kept[...] = picked.astype(jnp.bfloat16)
     ms_c[c] = jnp.broadcast_to(jnp.sum(picked * picked, axis=-1, keepdims=True), (cap, 128))
 
@@ -169,7 +193,7 @@
     total_square = exchange(ms_t, t, "tensor", T, mt_send, mt_recv)[:, :1]
     scale = lax.rsqrt(total_square / p.features + norm_eps)
     rows[me, a] = (
-        kept[...].astype(jnp.float32) * scale * gain[...].astype(jnp.float32)
+        kept[...].astype(jnp.float32) * scale * gain[...].astype(f32).reshape(1, width)
     ).astype(jnp.bfloat16)
 
     row_sent = []
@@ -226,9 +250,14 @@
     for m in range(1, p.mats):
         send_x(m, a, True, own=True)
 
-    fresh_ids = lax.broadcasted_iota(jnp.int32, (p.rows, p.rows), 1)
-    filler = (fresh_ids == fill_col[...]).astype(jnp.bfloat16)
-    out[...] = jnp.dot(filler, fresh[...], preferred_element_type=jnp.float32).astype(jnp.bfloat16)
+    base = lax.div(ids((1, p.rows), 1), batch) * batch
+    fresh_row = jnp.where(running > 0.5, -1, flat(refill[...]).astype(i32) + base)
+    filler = (ids((p.rows, p.rows), 0) == fresh_row).astype(bf16)
+    turned = (((0,), (0,)), ((), ()))
+    fetch[1].wait()
+    out[...] = lax.dot_general(filler, fresh[...], turned, preferred_element_type=f32).astype(bf16)
+    same = (ids((cap, cap), 0) == ids((cap, cap), 1)).astype(bf16)
+    spread[...] = lax.dot_general(picker[...], same, turned, preferred_element_type=f32).astype(bf16)
 
     def row_arrive_y(pairs):
         for slot, cond in pairs:
@@ -477,10 +506,14 @@
         h, i = column_part(n)
         columns = pl.ds(pl.multiple_of(i * fw + h * pw, pw), pw)
         settled = (kept[:, columns].astype(jnp.float32) + mine[n, a]).astype(jnp.bfloat16)
-        slots = lax.broadcasted_iota(jnp.int32, (p.rows, cap), 1)
-        spread = (slots == pick_col[...]).astype(jnp.bfloat16)
-        placed = jnp.dot(spread, settled, preferred_element_type=jnp.float32)
+        placed = jnp.dot(spread[...], settled, preferred_element_type=jnp.float32)
         out[:, columns] = (placed + out[:, columns].astype(jnp.float32)).astype(jnp.bfloat16)
+        write_out(n).start()
+
+    def write_out(n):
+        h, i = column_part(n)
+        columns = pl.ds(pl.multiple_of(i * fw + h * pw, pw), pw)
+        return pltpu.make_async_copy(out.at[:, columns], result.at[:, columns], out_sem.at[n])
 
     behind = 2
     for tick in range(p.parts + behind + R - 1):
@@ -525,6 +558,8 @@
         return carry
 
     lax.fori_loop(0, p.parts * R, settle, 0)
+    for n in range(p.parts):
+        write_out(n).wait()
 
 
 def make_body(mesh):
@@ -532,12 +567,6 @@
         p = Plan(mesh, states, gate_weight, down_weight)
         R, S, T, C, K = p.R, p.S, p.T, p.C, p.K
         cap, width, fw, hp, pw = p.cap, p.width, p.fw, p.hp, p.pw
-        running = halted.reshape(p.rows) == 0
-        slot_of = jnp.cumsum(running.astype(jnp.int32)) - 1
-        pick = jnp.where(running, slot_of, -1)
-        blocks, batch = refill_index.shape
-        base = lax.broadcasted_iota(jnp.int32, (blocks, batch), 0) * batch
-        fill = jnp.where(running, -1, (base + refill_index).reshape(p.rows))
         bf16, f32 = jnp.bfloat16, jnp.float32
         dma = lambda *shape: pltpu.SemaphoreType.DMA(shape)
         vmem = pl.BlockSpec(memory_space=pltpu.VMEM)
@@ -545,9 +574,14 @@
         return pl.pallas_call(
             functools.partial(block_kernel, p),
             out_shape=jax.ShapeDtypeStruct(states.shape, states.dtype),
-            in_specs=[vmem] * 6 + [hbm] * 3,
-            out_specs=vmem,
+            in_specs=[vmem] * 3 + [hbm] * 5,
+            out_specs=hbm,
             scratch_shapes=[
+                pltpu.VMEM((p.rows, width), bf16),
+                pltpu.VMEM((p.rows, width), bf16),
+                pltpu.VMEM((p.rows, width), bf16),
+                pltpu.VMEM((cap, p.rows), bf16),
+                pltpu.VMEM((p.rows, cap), bf16),
                 pltpu.VMEM((K, R, cap, width), bf16),
                 pltpu.VMEM((p.features, hp), bf16),
                 pltpu.VMEM((p.features, hp), bf16),
@@ -573,13 +607,13 @@
                 dma(p.parts, max(1, T - 1), R), dma(p.parts, max(1, T - 1), R),
                 dma(p.parts, R), dma(p.parts, R + 1),
                 pltpu.SemaphoreType.REGULAR,
+                dma(2), dma(p.parts),
             ],
             compiler_params=pltpu.CompilerParams(
                 collective_id=0, has_side_effects=True, vmem_limit_bytes=64000 * 1024
             ),
         )(
-            pick.reshape(1, p.rows), pick.reshape(p.rows, 1), fill.reshape(p.rows, 1),
-            states, fresh_rows, norm_gain.reshape(1, width), gate_weight, up_weight, down_weight,
+            halted, refill_index, norm_gain, states, fresh_rows, gate_weight, up_weight, down_weight,
         )
 
     return body

time: 256 us -> 248 us (0.969)
  other arithmetic: 3.31 us -> 0 us
where the time goes in v3:
time: 248 us; the launch traced here: 244 us
  Pallas kernels  242 us (98%)
    pallas_call x1, Pallas kernels, body(): pl.pallas_call(functools.partial(block_kernel, p), out_shape=jax.ShapeDty...  242 us

profile of v3, /device:TPU:8, one launch (start us, length us, event | category | flops | bytes accessed | tf_op | source)
XLA Modules:
  0.0 244.2 jit_solution(15972524062809423358)
XLA Ops:
  0.0 241.9 %shard_map.82 = bf16[512,1024]{1,0:T(8,128)(2,1)} custom-call(s32[8,64]{1,0:T(8,128)} %halted.1, s32[8,64]{1,0:T(8,128)} %refill.1, bf16[1024]{0:T(1024)(128)(2,1)} %gain.1, bf16[512,1024]{1,0:T(8,128)(2,1)} %states_in.1, bf16[512,1024]{1,0:T(8,128)(2,1)} %fresh_in.1, bf16[512,2048]{1,0:T(8,128)(2,1)} %gate_w.1, bf16[512,2048]{1,0:T(8,128)(2,1)} %up_w.1, ...), custom_call_target="tpu_custom_call" | custom-call | tf_op jit(solution)/shard_map/pallas_call | solution.py:574
  241.9 2.3 copy.10

commit v4 on v3

--- a/solution.py
+++ b/solution.py
@@ -25,7 +25,9 @@
         self.hp = gate.shape[1] // self.R
         self.halves = self.fw // 128
         self.pw = self.fw // self.halves
-        self.mats = 2 + self.halves
+        self.gates, self.ups = [0, 1], [2, 3]
+        self.down0 = 4
+        self.mats = self.down0 + self.halves
         self.parts = self.unit * self.halves
 
 
@@ -73,16 +75,22 @@
     by_distance = [(a, True)] + [pair for step in range(1, R) for pair in near(step)]
     arrivals = by_distance[1:]
 
+    gates, ups, down0 = p.gates, p.ups, p.down0
+    sub = fw // len(ups)
+
     def source_at(m, to):
-        if m < 2:
-            return (gate_w, up_w)[m].at[:, pl.ds(pl.multiple_of(to * hp, hp), hp)]
-        h = m - 2
-        return down_w.at[pl.ds(pl.multiple_of(to * hp, hp), hp), h * pw : (h + 1) * pw]
+        columns = pl.ds(pl.multiple_of(to * hp, hp), hp)
+        if m < down0:
+            k = m % len(ups)
+            return (gate_w if m in gates else up_w).at[k * sub : (k + 1) * sub, columns]
+        h = m - down0
+        return down_w.at[columns, h * pw : (h + 1) * pw]
 
     def full_at(m, owner):
-        if m < 2:
-            return (gate_full, up_full)[m].at[pl.ds(pl.multiple_of(owner * fw, fw), fw), :]
-        return down_full.at[m - 2, owner]
+        if m < down0:
+            span = pl.ds(pl.multiple_of(owner * fw + (m % len(ups)) * sub, sub), sub)
+            return (gate_full if m in gates else up_full).at[span, :]
+        return down_full.at[m - down0, owner]
 
     at_end = jnp.logical_or(a == 0, a == R - 1)
 
@@ -146,8 +154,10 @@
 
     far = list(range(2, R))
     close = range(1, min(R, 2))
-    send_z(0, close)
-    send_x(0, a, True, own=True)
+    for m in gates:
+        send_z(m, close)
+    for m in gates:
+        send_x(m, a, True, own=True)
     for m in range(p.mats):
         local(m).start()
 
@@ -244,10 +254,11 @@
 
     row_z(a, 1, a + 1 < R)
     row_z(a, -1, a > 0)
-    send_z(1, close, at_end)
+    for m in ups:
+        send_z(m, close, at_end)
     row_y(a, True)
     row_c(a, 0, True)
-    for m in range(1, p.mats):
+    for m in range(len(gates), p.mats):
         send_x(m, a, True, own=True)
 
     base = lax.div(ids((1, p.rows), 1), batch) * batch
@@ -288,12 +299,18 @@
     for step in range(1, min(R, 3)):
         row_step(step)
         if step == 1:
-            forward_z(0, near(1))
-    send_z(1, close, inner, lambda to: jnp.logical_and(to > 0, to < R - 1))
-    send_z(0, far, inner)
-    send_z(1, far, inner)
-    forward_z(0, only(near(2), at_end))
-    forward_z(1, only(near(2), at_end))
+            for m in gates:
+                forward_z(m, near(1))
+    for m in ups:
+        send_z(m, close, inner, lambda to: jnp.logical_and(to > 0, to < R - 1))
+    for m in gates:
+        send_z(m, far, inner)
+    for m in ups:
+        send_z(m, far, inner)
+    for m in gates:
+        forward_z(m, only(near(2), at_end))
+    for m in ups:
+        forward_z(m, only(near(2), at_end))
     if C > 1:
         @pl.when(at_end)
         def _():
@@ -303,21 +320,26 @@
                 )
             pl.semaphore_wait(pair_sem, C - 1)
 
-    for m in range(2):
+    for m in (*gates, *ups):
         send_z(m, far[:1], at_end)
     for step in beyond:
         row_step(step)
-    for m in range(2):
+    for m in (*gates, *ups):
         send_z(m, beyond, at_end)
-    for h in range(p.halves):
-        send_z(2 + h, close, at_end)
-    send_z(2, far, at_end)
+    send_z(down0, close, at_end)
+    send_z(down0, far, at_end)
+    for h in range(1, p.halves):
+        send_z(down0 + h, close, at_end)
     row_arrive_y(by_distance[:3])
-    forward_z(1, only(near(1), inner))
+    for m in ups:
+        forward_z(m, only(near(1), inner))
     row_arrive_y(by_distance[3:])
-    send_z(1, close, inner, lambda to: jnp.logical_or(to == 0, to == R - 1))
-    forward_z(1, only(near(1), at_end))
-    forward_z(0, only(near(2), inner))
+    for m in ups:
+        send_z(m, close, inner, lambda to: jnp.logical_or(to == 0, to == R - 1))
+    for m in ups:
+        forward_z(m, only(near(1), at_end))
+    for m in gates:
+        forward_z(m, only(near(2), inner))
     for slot in range(R):
         for tstep in range(T):
             for step in range(1, C):
@@ -327,8 +349,8 @@
                     "dp", (c + C - step) % C,
                 ).wait_recv()
     for h in range(p.halves):
-        send_z(2 + h, close, inner)
-        send_z(2 + h, far, inner)
+        send_z(down0 + h, close, inner)
+        send_z(down0 + h, far, inner)
 
     per_owner = S // p.unit
     for m in range(p.mats):
@@ -349,22 +371,26 @@
         for frm, cond in pairs:
             def run(frm=frm, first=cond is True):
                 for step in range(1, S):
-                    wait_x(m, frm, step)
+                    for piece in ups if m else gates:
+                        wait_x(piece, frm, step)
                 for k in range(per_owner):
                     product_block(frm * per_owner + k, weights, acc, first and k == 0)
             when(cond, run)
 
     products(0, by_distance[:1])
     products(0, near(1))
-    forward_z(1, only(near(2), inner))
+    for m in ups:
+        forward_z(m, only(near(2), inner))
     products(0, only(near(2), at_end))
     for step in beyond:
-        forward_z(0, near(step))
+        for m in gates:
+            forward_z(m, near(step))
     products(1, by_distance[:1])
     products(1, only(near(2), at_end))
     products(1, near(1))
     for step in beyond:
-        forward_z(1, near(step))
+        for m in ups:
+            forward_z(m, near(step))
         products(0, near(step))
     products(0, only(near(2), inner))
     products(1, only(near(2), inner))
@@ -421,7 +447,7 @@
 
     def part_a(n):
         h, turn = n // p.unit, n % p.unit
-        m = 2 + h
+        m = down0 + h
         if turn == 0:
             forward_z(m, arrivals)
             if h + 1 < p.halves:

time: 248 us -> 245 us (0.988)
  Pallas kernels: 242 us -> 238 us
    pallas_call x1, Pallas kernels: 242 us -> 238 us  [body(): pl.pallas_call(functools.partial(block_kernel, p), out_shape=jax.ShapeDty...]
where the time goes in v4:
time: 245 us; the launch traced here: 240 us
  Pallas kernels  238 us (97%)
    pallas_call x1, Pallas kernels, body(): pl.pallas_call(functools.partial(block_kernel, p), out_shape=jax.ShapeDty...  238 us

profile of v4, /device:TPU:8, one launch (start us, length us, event | category | flops | bytes accessed | tf_op | source)
XLA Modules:
  0.0 240.4 jit_solution(17370746041383392716)
XLA Ops:
  0.0 238.2 %shard_map.82 = bf16[512,1024]{1,0:T(8,128)(2,1)} custom-call(s32[8,64]{1,0:T(8,128)} %halted.1, s32[8,64]{1,0:T(8,128)} %refill.1, bf16[1024]{0:T(1024)(128)(2,1)} %gain.1, bf16[512,1024]{1,0:T(8,128)(2,1)} %states_in.1, bf16[512,1024]{1,0:T(8,128)(2,1)} %fresh_in.1, bf16[512,2048]{1,0:T(8,128)(2,1)} %gate_w.1, bf16[512,2048]{1,0:T(8,128)(2,1)} %up_w.1, ...), custom_call_target="tpu_custom_call" | custom-call | tf_op jit(solution)/shard_map/pallas_call | solution.py:600
  238.2 2.3 copy.10

commit v5 on v4

--- a/solution.py
+++ b/solution.py
@@ -457,6 +457,7 @@
                 if (step + turn) % p.unit == 0:
                     wait_x(m, frm, step)
 
+    def part_a_products(n, low, high):
         def body(index, carry):
             tstep, slot = index // R, slot_at(index % R)
             for step in range(1, C):
@@ -466,7 +467,7 @@
                 out_c(n, tstep, slot, step).start()
             return carry
 
-        lax.fori_loop(0, T * R, body, 0)
+        lax.fori_loop(low, high, body, 0)
 
     def chip_sum(n, tstep, slot):
         value = product(n, slot, ((t + 1 + tstep) % T) * C + c)
@@ -545,7 +546,9 @@
     for tick in range(p.parts + behind + R - 1):
         if tick < p.parts:
             part_a(tick)
+            part_a_products(tick, 0, (T - 1) * R)
             part_b(tick, 0, R)
+            part_a_products(tick, (T - 1) * R, T * R)
         if 0 <= tick - behind < p.parts:
             part_c(tick - behind, 0, R)
         for hop in range(1, R - 1):

time: 245 us -> 248 us (1.012)
  Pallas kernels: 238 us -> 243 us
    pallas_call x1, Pallas kernels: 238 us -> 243 us  [body(): pl.pallas_call(functools.partial(block_kernel, p), out_shape=jax.ShapeDty...]
where the time goes in v5:
time: 248 us; the launch traced here: 245 us
  Pallas kernels  243 us (98%)
    pallas_call x1, Pallas kernels, body(): pl.pallas_call(functools.partial(block_kernel, p), out_shape=jax.ShapeDty...  243 us

profile of v5, /device:TPU:8, one launch (start us, length us, event | category | flops | bytes accessed | tf_op | source)
XLA Modules:
  0.0 244.9 jit_solution(14116512575533298358)
XLA Ops:
  0.0 242.6 %shard_map.82 = bf16[512,1024]{1,0:T(8,128)(2,1)} custom-call(s32[8,64]{1,0:T(8,128)} %halted.1, s32[8,64]{1,0:T(8,128)} %refill.1, bf16[1024]{0:T(1024)(128)(2,1)} %gain.1, bf16[512,1024]{1,0:T(8,128)(2,1)} %states_in.1, bf16[512,1024]{1,0:T(8,128)(2,1)} %fresh_in.1, bf16[512,2048]{1,0:T(8,128)(2,1)} %gate_w.1, bf16[512,2048]{1,0:T(8,128)(2,1)} %up_w.1, ...), custom_call_target="tpu_custom_call" | custom-call | tf_op jit(solution)/shard_map/pallas_call | solution.py:603
  242.6 2.3 copy.10
